TPU v7x, 32 devices: a whole 2x2x4 slice. The times are simulated.
32 devices in a mesh: pp: 4 (over y, x), cp: 2 (over core), tp: 4 (over z).
Axes of the slice: x: 2, y: 2, z: 4, core: 2. Of those that a mesh axis runs over, the one named last changes fastest.
Arguments:
- query: bfloat16 [4, 384, 8192], P('pp', 'cp', 'tp'), may hold values from -125 to 125
- keys: bfloat16 [4, 384, 512], P('pp', 'cp', 'tp'), may hold values from -5 to 5
- values: bfloat16 [4, 384, 512], P('pp', 'cp', 'tp'), may hold values from -6 to 6
- attn_out: bfloat16 [4, 384, 8192], P('pp', 'cp', 'tp'), may hold values from -6 to 6
- grad_out: bfloat16 [4, 384, 8192], P('pp', 'cp', 'tp'), may hold values from -192 to 192
- span_pairs: int32 [2, 2], replicated, may hold values from 0 to 3, as said below
Outputs:
- key_grad: bfloat16 [4, 384, 512], P('pp', 'cp', 'tp')
- value_grad: bfloat16 [4, 384, 512], P('pp', 'cp', 'tp')
- upstream_grad: bfloat16 [4, 384, 8192], P('pp', 'cp', 'tp')
Inputs may be any that keep to these rules, and one draw needn't show every extreme that they name: `span_pairs`: row r names the two spans of 96 positions held by context rank r, in either order; every span is named once.
All inputs are finite; a program needn't handle non-finite values.
Results may differ from a plain program's by a relative error of at most 0.0052.
Values may be sent and summed in bfloat16 or wider, within the bound.
A program may use at most 64 MiB of HBM per device.

v0:
```python
import math

import jax
import jax.numpy as jnp
from jax import lax
from jax.sharding import PartitionSpec as P


def shifted(block, axis, distance):
    devices = range(lax.axis_size(axis))
    route = [(i - distance, i) for i in devices if i - distance in devices]
    return lax.ppermute(block, axis, route)


def grad_block(
    query_rows,
    grad_rows,
    lse_rows,
    delta_rows,
    query_pos,
    key_block,
    value_block,
    key_pos,
    scale_factor,
):
    score = (
        jnp.einsum("qhd,kd->hqk", query_rows, key_block, preferred_element_type=jnp.float32)
        * scale_factor
    )
    kept = (key_pos[None, :] <= query_pos[:, None])[None]
    prob = jnp.exp(jnp.where(kept, score - lse_rows[:, :, None], -jnp.inf))
    prob_low = prob.astype(jnp.bfloat16)
    dprob = jnp.einsum("qhd,kd->hqk", grad_rows, value_block, preferred_element_type=jnp.float32)
    dscore = (prob * (dprob - delta_rows[:, :, None]) * scale_factor).astype(jnp.bfloat16)
    query_term = jnp.einsum("hqk,kd->qhd", dscore, key_block, preferred_element_type=jnp.float32)
    key_term = jnp.einsum("hqk,qhd->kd", dscore, query_rows, preferred_element_type=jnp.float32)
    value_term = jnp.einsum("hqk,qhd->kd", prob_low, grad_rows, preferred_element_type=jnp.float32)
    return (query_term, jnp.concatenate([key_term, value_term], axis=1))


def body(query, keys, values, attn_out, grad_out, span_pairs):
    head_dim = keys.shape[2]
    row_count = query.shape[1]
    span_len = row_count // 2
    head_count = query.shape[2] // head_dim
    rank_total = lax.axis_size("cp")
    my_rank = lax.axis_index("cp")
    seq_len = row_count * rank_total
    block_len = min(512, seq_len)
    block_total = seq_len // block_len
    scale_factor = 1.0 / math.sqrt(head_dim)
    flat_ids = span_pairs.reshape(-1)
    slot_ids = jnp.arange(flat_ids.shape[0], dtype=jnp.int32)
    matches = (flat_ids[:, None] == slot_ids[None, :]).astype(jnp.int32)
    slot_of = jnp.sum(matches * slot_ids[:, None], axis=0)
    my_spans = lax.dynamic_index_in_dim(span_pairs, my_rank, 0, keepdims=False)
    key_gathered, value_gathered = (
        lax.all_gather(keys[0], "cp", axis=0, tiled=True),
        lax.all_gather(values[0], "cp", axis=0, tiled=True),
    )
    key_sorted = jnp.take(
        key_gathered.reshape(2 * rank_total, span_len, head_dim), slot_of, axis=0
    ).reshape(seq_len, head_dim)
    value_sorted = jnp.take(
        value_gathered.reshape(2 * rank_total, span_len, head_dim), slot_of, axis=0
    ).reshape(seq_len, head_dim)
    query_parts = query[0].reshape(2, span_len, head_count, head_dim)
    grad_parts = grad_out[0].reshape(2, span_len, head_count, head_dim)
    output_parts = attn_out[0].reshape(2, span_len, head_count, head_dim)
    query_positions = [
        my_spans[part_index] * span_len + jnp.arange(span_len, dtype=jnp.int32)
        for part_index in range(2)
    ]

    def block_limit():
        return block_total

    lse_list = []
    delta_list = []
    for part_index in range(2):
        query_rows = query_parts[part_index]
        query_pos = query_positions[part_index]

        def stats_step(block_index, carry):
            top_now, mass_now = carry
            start = block_index * block_len
            key_block = lax.dynamic_slice_in_dim(key_sorted, start, block_len, 0)
            key_pos = start + jnp.arange(block_len, dtype=jnp.int32)
            score = (
                jnp.einsum("qhd,kd->hqk", query_rows, key_block, preferred_element_type=jnp.float32)
                * scale_factor
            )
            score = jnp.where((key_pos[None, :] <= query_pos[:, None])[None], score, -jnp.inf)
            top_next = jnp.maximum(top_now, jnp.max(score, axis=-1))
            mass_next = mass_now * jnp.exp(top_now - top_next) + jnp.sum(
                jnp.exp(score - top_next[:, :, None]), axis=-1
            )
            return (top_next, mass_next)

        start_top = jnp.full((head_count, span_len), -1e30, jnp.float32)
        start_mass = jnp.zeros((head_count, span_len), jnp.float32)
        top_final, mass_final = lax.fori_loop(0, block_limit(), stats_step, (start_top, start_mass))
        lse_list.append(top_final + jnp.log(mass_final))
        delta_list.append(
            jnp.einsum(
                "qhd,qhd->hq",
                grad_parts[part_index],
                output_parts[part_index],
                preferred_element_type=jnp.float32,
            )
        )
    pair_acc = jnp.zeros((seq_len, 2 * head_dim), jnp.float32)
    query_grads = []
    for part_index in range(2):
        query_rows = query_parts[part_index]
        grad_rows = grad_parts[part_index]
        lse_rows = lse_list[part_index]
        delta_rows = delta_list[part_index]
        query_pos = query_positions[part_index]

        def grad_step(block_index, carry):
            query_acc, pair_now = carry
            start = block_index * block_len
            key_block = lax.dynamic_slice_in_dim(key_sorted, start, block_len, 0)
            value_block = lax.dynamic_slice_in_dim(value_sorted, start, block_len, 0)
            key_pos = start + jnp.arange(block_len, dtype=jnp.int32)
            query_term, pair_term = grad_block(
                query_rows,
                grad_rows,
                lse_rows,
                delta_rows,
                query_pos,
                key_block,
                value_block,
                key_pos,
                scale_factor,
            )
            previous = lax.dynamic_slice_in_dim(pair_now, start, block_len, 0)
            pair_now = lax.dynamic_update_slice_in_dim(pair_now, previous + pair_term, start, 0)
            return (query_acc + query_term, pair_now)

        query_start = jnp.zeros((span_len, head_count, head_dim), jnp.float32)
        query_acc, pair_acc = lax.fori_loop(0, block_limit(), grad_step, (query_start, pair_acc))
        query_low = query_acc.reshape(span_len, head_count * head_dim).astype(jnp.bfloat16)
        query_grads.append(query_low)
    upstream = jnp.concatenate(query_grads, axis=0)
    upstream = shifted(upstream, "pp", -1)
    pair_rank = jnp.take(
        pair_acc.reshape(2 * rank_total, span_len, 2 * head_dim), flat_ids, axis=0
    ).reshape(seq_len, 2 * head_dim)
    owned = lax.psum_scatter(pair_rank, "cp", scatter_dimension=0, tiled=True)
    key_grad = owned[:, :head_dim].astype(jnp.bfloat16)[None]
    value_grad = owned[:, head_dim:].astype(jnp.bfloat16)[None]
    return (key_grad, value_grad, upstream[None])


def solution(mesh):
    in_specs = (
        P("pp", "cp", "tp"),
        P("pp", "cp", "tp"),
        P("pp", "cp", "tp"),
        P("pp", "cp", "tp"),
        P("pp", "cp", "tp"),
        P(),
    )
    out_specs = (P("pp", "cp", "tp"), P("pp", "cp", "tp"), P("pp", "cp", "tp"))
    return jax.shard_map(body, mesh=mesh, in_specs=in_specs, out_specs=out_specs, check_vma=False)
```

profile of v0, /device:TPU:0, one launch (start us, length us, event | category | flops | bytes accessed | tf_op | source)
XLA Modules:
  0.0 75.3 jit_solution(15705135370273473845)
XLA Ops:
  7.2 0.8 %reshape.173 = s32[4]{0:T(128)S(1)} reshape(s32[2,2]{1,0:T(2,128)} %param.13) | data formatting | bytes 32 | tf_op jit(solution)/shard_map/reshape | solution.py:52
  8.2 0.7 constant_dynamic-slice_fusion
  10.2 0.7 iota_compare_fusion.3
  11.7 0.7 iota_compare_fusion.1
  12.4 2.2 %all-gather = bf16[1,384,128]{2,1,0:T(8,128)(2,1)S(1)} all-gather(bf16[1,192,128]{2,1,0:T(8,128)(2,1)} %param.9), channel_id=2, replica_groups=mesh['pp'=4,'cp'=2,'tp'=4] {'cp'}, dimensions={1}, use_global_device_ids=true | all-gather | bytes 147456 | tf_op jit(solution)/shard_map/all_gather | solution.py:58
  14.6 2.1 %all-gather.1 = bf16[1,384,128]{2,1,0:T(8,128)(2,1)S(1)} all-gather(bf16[1,192,128]{2,1,0:T(8,128)(2,1)} %param.10), channel_id=3, replica_groups=mesh['pp'=4,'cp'=2,'tp'=4] {'cp'}, dimensions={1}, use_global_device_ids=true | all-gather | bytes 147456 | tf_op jit(solution)/shard_map/all_gather | solution.py:59
  17.8 1.2 %slice_bitcast_fusion.2 = (bf16[12,8,16,128]{3,1,2,0:T(8,128)(2,1)S(1)}, bf16[12,8,16,128]{3,1,2,0:T(8,128)(2,1)S(1)}) fusion(bf16[1,192,2048]{2,1,0:T(8,128)(2,1)} %param.8), kind=kLoop, calls=%fused_computation.76 | loop fusion | bytes 1572864
  19.4 1.0 %copy-done.13 = bf16[1,192,2048]{2,1,0:T(8,128)(2,1)S(1)} copy-done((bf16[1,192,2048]{2,1,0:T(8,128)(2,1)S(1)}, bf16[1,192,2048]{2,1,0:T(8,128)(2,1)}, u32[]{:S(2)}) %copy-start.13) | copy-done | bytes 786456
  21.0 0.8 %copy-done.3 = bf16[12,8,16,128]{3,2,1,0:T(8,128)(2,1)} copy-done((bf16[12,8,16,128]{3,2,1,0:T(8,128)(2,1)}, bf16[12,8,16,128]{3,2,1,0:T(8,128)(2,1)S(1)}, u32[]{:S(2)}) %copy-start.3) | copy-done | bytes 393240
  22.2 0.7 fusion.20
  23.0 0.9 %exponential_reduce_fusion.1 = f32[16,96]{1,0:T(8,128)S(1)} fusion(f32[384,96,16]{0,1,2:T(8,128)S(1)} %get-tuple-element.107, f32[16,96]{1,0:T(8,128)S(1)} %broadcast_maximum_fusion.1, pred[96,384]{1,0:T(8,128)(4,1)S(1)} %iota_compare_fusion.2), kind=kLoop, calls=%fused_computation.34 | loop fusion | flops 2357760 | bytes 2408448 | tf_op jit(solution)/shard_map/while/body/eval_jaxpr/reduce_sum | solution.py:95
  23.9 0.7 fusion.21
  24.7 0.9 %exponential_reduce_fusion = f32[16,96]{1,0:T(8,128)S(1)} fusion(f32[384,96,16]{0,1,2:T(8,128)S(1)} %get-tuple-element.110, f32[16,96]{1,0:T(8,128)S(1)} %broadcast_maximum_fusion, pred[96,384]{1,0:T(8,128)(4,1)S(1)} %iota_compare_fusion), kind=kLoop, calls=%fused_computation.33 | loop fusion | flops 2357760 | bytes 2408448 | tf_op jit(solution)/shard_map/while/body/eval_jaxpr/reduce_sum | solution.py:95
  25.6 1.3 %fusion.8 = (bf16[384,16,96]{0,2,1:T(8,128)(2,1)S(1)}, bf16[384,16,96]{0,2,1:T(8,128)(2,1)S(1)}, f32[384,96,16]{0,1,2:T(8,128)S(1)}) fusion(f32[384,96,16]{0,1,2:T(8,128)S(1)} %get-tuple-element.110, f32[16,96]{1,0:T(8,128)S(1)} %copy.52, f32[16,96]{1,0:T(8,128)S(1)} %log_add_fusion, pred[384,96]{0,1:T(8,128)(4,1)S(1)} %copy-done.19, ...), kind=kOutput, calls=%fused_computation.14 | convolution fusion | flops 155713536 | bytes 7618560 | tf_op jit(solution)/shard_map/while/body/eval_jaxpr/qhd,kd->hqk/dot_general | solution.py:33
  27.0 1.2 %fusion.33 = bf16[16,12,8,128]{3,2,1,0:T(8,128)(2,1)S(1)} fusion(bf16[384,128,1]{1,0,2:T(8,128)(2,1)S(1)} %bitcast.201, f32[384,96,16]{0,1,2:T(8,128)S(1)} %get-tuple-element.122, f32[384,96,16]{0,1,2:T(8,128)S(1)} %get-tuple-element.110, f32[16,96]{1,0:T(8,128)S(1)} %copy.52, f32[16,96]{1,0:T(8,128)S(1)} %log_add_fusion, pred[96,384]{1,0:T(8,128)(4,1)S(1)} %copy-done.17), kind=kOutput, calls=%fused_computation.50 | convolution fusion | flops 155320320 | bytes 5259264 | tf_op jit(solution)/shard_map/while/body/eval_jaxpr/hqk,kd->qhd/dot_general | solution.py:35
  28.2 2.0 %fusion.15 = (bf16[384,16,96]{0,2,1:T(8,128)(2,1)}, bf16[384,16,96]{0,2,1:T(8,128)(2,1)S(1)}, f32[384,96,16]{0,1,2:T(8,128)S(1)}) fusion(f32[384,96,16]{0,1,2:T(8,128)S(1)} %get-tuple-element.107, f32[16,96]{1,0:T(8,128)S(1)} %copy.43, f32[16,96]{1,0:T(8,128)S(1)} %log_add_fusion.1, pred[384,96]{0,1:T(8,128)(4,1)S(1)} %copy-done.18, ...), kind=kOutput, calls=%fused_computation.25 | convolution fusion | flops 155713536 | bytes 7618560 | tf_op jit(solution)/shard_map/while/body/eval_jaxpr/qhd,kd->hqk/dot_general | solution.py:33
  30.2 1.1 %fusion.32 = bf16[16,12,8,128]{3,2,1,0:T(8,128)(2,1)S(1)} fusion(bf16[384,128,1]{1,0,2:T(8,128)(2,1)S(1)} %bitcast.202, f32[384,96,16]{0,1,2:T(8,128)S(1)} %get-tuple-element.108, f32[384,96,16]{0,1,2:T(8,128)S(1)} %get-tuple-element.107, f32[16,96]{1,0:T(8,128)S(1)} %copy.43, f32[16,96]{1,0:T(8,128)S(1)} %log_add_fusion.1, pred[96,384]{1,0:T(8,128)(4,1)S(1)} %copy-done.15), kind=kOutput, calls=%fused_computation.49 | convolution fusion | flops 155320320 | bytes 5259264 | tf_op jit(solution)/shard_map/while/body/eval_jaxpr/hqk,kd->qhd/dot_general | solution.py:35
  31.5 0.9 %pad_maximum_fusion = bf16[192,2048]{1,0:T(8,128)(2,1)} fusion(bf16[96,2048]{1,0:T(8,128)(2,1)S(1)} %get-tuple-element.123, bf16[96,2048]{1,0:T(8,128)(2,1)S(1)} %get-tuple-element.124), kind=kLoop, calls=%fused_computation.57 | loop fusion | flops 1572864 | bytes 1572864 | tf_op jit(solution)/shard_map/concatenate | solution.py:146
  32.4 1.5 %collective-permute-start = (bf16[192,2048]{1,0:T(8,128)(2,1)}, bf16[192,2048]{1,0:T(8,128)(2,1)}, u32[]{:S(2)}, u32[]{:S(2)}) collective-permute-start(bf16[192,2048]{1,0:T(8,128)(2,1)} %pad_maximum_fusion), channel_id=1, source_target_pairs={{8,0},{16,8},{24,16},{9,1},{17,9},{25,17},{10,2},{18,10},{26,18},{... | collective-permute-start | bytes 2359304 | tf_op jit(solution)/shard_map/ppermute | solution.py:12
  34.2 2.1 %dot_general.68 = bf16[4,96,16,96]{1,0,3,2:T(4,128)(2,1)} reshape(bf16[384,16,96]{0,2,1:T(8,128)(2,1)S(1)} %get-tuple-element.79) | data formatting | bytes 2359296 | tf_op jit(solution)/shard_map/while/body/eval_jaxpr/hqk,qhd->kd/dot_general | solution.py:36
  36.3 2.1 %dot_general.70 = bf16[4,96,16,96]{1,0,3,2:T(4,128)(2,1)} reshape(bf16[384,16,96]{0,2,1:T(8,128)(2,1)S(1)} %get-tuple-element.80) | data formatting | bytes 2359296 | tf_op jit(solution)/shard_map/while/body/eval_jaxpr/hqk,qhd->kd/dot_general | solution.py:37
  38.4 2.1 %dot_general.61 = bf16[4,96,16,96]{1,0,3,2:T(4,128)(2,1)} reshape(bf16[384,16,96]{0,2,1:T(8,128)(2,1)S(1)} %copy-done) | data formatting | bytes 2359296 | tf_op jit(solution)/shard_map/while/body/eval_jaxpr/hqk,qhd->kd/dot_general | solution.py:36
  40.4 1.2 %dot_general.63 = bf16[4,96,16,96]{1,0,3,2:T(4,128)(2,1)S(1)} reshape(bf16[384,16,96]{0,2,1:T(8,128)(2,1)S(1)} %get-tuple-element.82) | data formatting | bytes 2359296 | tf_op jit(solution)/shard_map/while/body/eval_jaxpr/hqk,qhd->kd/dot_general | solution.py:37
  41.7 3.4 %fusion.44 = f32[4,96,128]{2,1,0:T(8,128)S(1)} fusion(bf16[96,16,128,1]{2,1,0,3:T(8,128)(2,1)S(1)} %bitcast.208, bf16[4,96,16,96]{1,0,3,2:T(4,128)(2,1)} %dot_general.68), kind=kOutput, calls=%fused_computation.55 | convolution fusion | flops 150994944 | bytes 1769472 | tf_op jit(solution)/shard_map/while/body/eval_jaxpr/hqk,qhd->kd/dot_general | solution.py:36
  45.1 1.9 %fusion.47 = f32[4,96,128]{2,1,0:T(8,128)S(1)} fusion(bf16[96,16,128,1]{2,1,0,3:T(8,128)(2,1)S(1)} %bitcast.195, bf16[4,96,16,96]{1,0,3,2:T(4,128)(2,1)S(1)} %copy-done.7), kind=kOutput, calls=%fused_computation.56 | convolution fusion | flops 150994944 | bytes 1769472 | tf_op jit(solution)/shard_map/while/body/eval_jaxpr/hqk,qhd->kd/dot_general | solution.py:37
  47.1 1.9 %fusion.38 = f32[4,96,128]{2,1,0:T(8,128)S(1)} fusion(bf16[96,16,128,1]{2,1,0,3:T(8,128)(2,1)S(1)} %bitcast.206, bf16[4,96,16,96]{1,0,3,2:T(4,128)(2,1)S(1)} %copy-done.6), kind=kOutput, calls=%fused_computation.53 | convolution fusion | flops 150994944 | bytes 1769472 | tf_op jit(solution)/shard_map/while/body/eval_jaxpr/hqk,qhd->kd/dot_general | solution.py:36
  49.0 1.9 %fusion.41 = f32[4,96,128]{2,1,0:T(8,128)S(1)} fusion(bf16[96,16,128,1]{2,1,0,3:T(8,128)(2,1)S(1)} %bitcast.198, bf16[4,96,16,96]{1,0,3,2:T(4,128)(2,1)S(1)} %dot_general.63), kind=kOutput, calls=%fused_computation.54 | convolution fusion | flops 150994944 | bytes 1769472 | tf_op jit(solution)/shard_map/while/body/eval_jaxpr/hqk,qhd->kd/dot_general | solution.py:37
  51.6 0.9 %bitcast_select_fusion.2 = f32[384,256]{1,0:T(8,128)} fusion(f32[4,96,256]{2,1,0:T(8,128)S(1)} %gather_fusion, pred[384]{0:T(512)(128)(4,1)S(1)} %broadcast_in_dim.120), kind=kLoop, calls=%fused_computation.65 | loop fusion | flops 98304 | bytes 786816 | tf_op jit(solution)/shard_map/jit(_take)/select_n | solution.py:148
  52.5 2.8 %collective-permute-done = bf16[192,2048]{1,0:T(8,128)(2,1)} collective-permute-done((bf16[192,2048]{1,0:T(8,128)(2,1)}, bf16[192,2048]{1,0:T(8,128)(2,1)}, u32[]{:S(2)}, u32[]{:S(2)}) %collective-permute-start) | collective-permute-done | bytes 786464 | tf_op jit(solution)/shard_map/ppermute | solution.py:12
  55.3 9.5 %reduce-scatter.2.cloned.1.call-done = f32[192,256]{1,0:T(8,128)} async-done(((f32[384,256]{1,0:T(8,128)}), f32[192,256]{1,0:T(8,128)}) %reduce-scatter.2.cloned.1.call-update) | async-done | bytes 196624 | tf_op jit(solution)/shard_map/reduce_scatter | solution.py:151
  64.8 0.9 %convert.4 = bf16[192,256]{1,0:T(8,128)(2,1)S(1)} convert(f32[192,256]{1,0:T(8,128)} %reduce-scatter.2.cloned.1.call-done) | non-fusion elementwise | flops 49152 | bytes 294912 | tf_op jit(solution)/shard_map/convert.1
  66.4 2.1 %copy.104 = bf16[1,192,2048]{2,1,0:T(8,128)(2,1)} copy(bf16[1,192,2048]{2,1,0:T(8,128)(2,1)} %bitcast.36) | data formatting | bytes 1572864
  (84 shorter events, 5.1 us)
Async XLA Ops:
  7.2 12.0 %copy-start.12 = (bf16[1,192,2048]{2,1,0:T(8,128)(2,1)S(1)}, bf16[1,192,2048]{2,1,0:T(8,128)(2,1)}, u32[]{:S(2)}) copy-start(bf16[1,192,2048]{2,1,0:T(8,128)(2,1)} %param.11) | copy-start | bytes 2359300
  7.2 57.7 %reduce-scatter.2.cloned.1.call-start = ((), (), s32[]{:S(2)}) async-start(), calls=%async_computation.1 | async-start | bytes 589824 | tf_op jit(solution)/shard_map/reduce_scatter | solution.py:151
  8.0 2.0 %copy-start.21 = (s32[4]{0:T(128)}, s32[4]{0:T(128)S(1)}, u32[]{:S(2)}) copy-start(s32[4]{0:T(128)S(1)} %reshape.173) | copy-start | bytes 52
  10.2 12.8 %copy-start.14 = (pred[96,384]{1,0:T(8,128)(4,1)}, pred[96,384]{1,0:T(8,128)(4,1)S(1)}, u32[]{:S(2)}) copy-start(pred[96,384]{1,0:T(8,128)(4,1)S(1)} %iota_compare_fusion.2) | copy-start | bytes 110596
  11.7 13.0 %copy-start.16 = (pred[96,384]{1,0:T(8,128)(4,1)}, pred[96,384]{1,0:T(8,128)(4,1)S(1)}, u32[]{:S(2)}) copy-start(pred[96,384]{1,0:T(8,128)(4,1)S(1)} %iota_compare_fusion) | copy-start | bytes 110596
  19.0 1.4 %copy-start.13 = (bf16[1,192,2048]{2,1,0:T(8,128)(2,1)S(1)}, bf16[1,192,2048]{2,1,0:T(8,128)(2,1)}, u32[]{:S(2)}) copy-start(bf16[1,192,2048]{2,1,0:T(8,128)(2,1)} %param.12) | copy-start | bytes 2359300
  19.1 4.8 %copy-start.10 = (bf16[12,8,16,128]{3,2,1,0:T(8,128)(2,1)}, bf16[12,8,16,128]{3,2,1,0:T(8,128)(2,1)S(1)}, u32[]{:S(2)}) copy-start(bf16[12,8,16,128]{3,2,1,0:T(8,128)(2,1)S(1)} %copy.64) | copy-start | bytes 1179652
  19.2 3.0 %copy-start.8 = (bf16[12,8,16,128]{3,2,1,0:T(8,128)(2,1)}, bf16[12,8,16,128]{3,2,1,0:T(8,128)(2,1)S(1)}, u32[]{:S(2)}) copy-start(bf16[12,8,16,128]{3,2,1,0:T(8,128)(2,1)S(1)} %copy.59) | copy-start | bytes 1179652
  20.6 5.0 %copy-start.1 = (bf16[12,8,16,128]{3,2,1,0:T(8,128)(2,1)}, bf16[12,8,16,128]{3,2,1,0:T(8,128)(2,1)S(1)}, u32[]{:S(2)}) copy-start(bf16[12,8,16,128]{3,2,1,0:T(8,128)(2,1)S(1)} %copy.65) | copy-start | bytes 1179652
  21.0 0.8 %copy-start.3 = (bf16[12,8,16,128]{3,2,1,0:T(8,128)(2,1)}, bf16[12,8,16,128]{3,2,1,0:T(8,128)(2,1)S(1)}, u32[]{:S(2)}) copy-start(bf16[12,8,16,128]{3,2,1,0:T(8,128)(2,1)S(1)} %copy.60) | copy-start | bytes 1179652
  23.9 1.7 %copy-start.19 = (pred[384,96]{0,1:T(8,128)(4,1)S(1)}, pred[384,96]{0,1:T(8,128)(4,1)}, u32[]{:S(2)}) copy-start(pred[384,96]{0,1:T(8,128)(4,1)} %iota_compare_fusion.1) | copy-start | bytes 110596
  25.6 1.4 %copy-start.17 = (pred[96,384]{1,0:T(8,128)(4,1)S(1)}, pred[96,384]{1,0:T(8,128)(4,1)}, u32[]{:S(2)}) copy-start(pred[96,384]{1,0:T(8,128)(4,1)} %copy-done.16) | copy-start | bytes 110596
  27.0 1.2 %copy-start.4 = (bf16[12,8,16,128]{3,2,1,0:T(8,128)(2,1)S(1)}, bf16[12,8,16,128]{3,2,1,0:T(8,128)(2,1)}, u32[]{:S(2)}) copy-start(bf16[12,8,16,128]{3,2,1,0:T(8,128)(2,1)} %copy-done.3) | copy-start | bytes 1179652
  27.0 1.2 %copy-start.18 = (pred[384,96]{0,1:T(8,128)(4,1)S(1)}, pred[384,96]{0,1:T(8,128)(4,1)}, u32[]{:S(2)}) copy-start(pred[384,96]{0,1:T(8,128)(4,1)} %iota_compare_fusion.3) | copy-start | bytes 110596
  28.2 2.0 %copy-start.15 = (pred[96,384]{1,0:T(8,128)(4,1)S(1)}, pred[96,384]{1,0:T(8,128)(4,1)}, u32[]{:S(2)}) copy-start(pred[96,384]{1,0:T(8,128)(4,1)} %copy-done.14) | copy-start | bytes 110596
  31.4 2.5 %copy-start.22 = (s32[4]{0:T(128)S(1)}, s32[4]{0:T(128)}, u32[]{:S(2)}) copy-start(s32[4]{0:T(128)} %copy-done.21) | copy-start | bytes 52
  31.4 2.5 %copy-start.20 = (s32[2,2]{1,0:T(2,128)S(1)}, s32[2,2]{1,0:T(2,128)}, u32[]{:S(2)}) copy-start(s32[2,2]{1,0:T(2,128)} %param.13) | copy-start | bytes 52
  32.4 22.9 %collective-permute-start = (bf16[192,2048]{1,0:T(8,128)(2,1)}, bf16[192,2048]{1,0:T(8,128)(2,1)}, u32[]{:S(2)}, u32[]{:S(2)}) collective-permute-start(bf16[192,2048]{1,0:T(8,128)(2,1)} %pad_maximum_fusion), channel_id=1, source_target_pairs={{8,0},{16,8},{24,16},{9,1},{17,9},{25,17},{10,2},{18,10},{26,18},{... | collective-permute-start | bytes 2359304 | tf_op jit(solution)/shard_map/ppermute | solution.py:12
  36.3 2.1 %copy-start = (bf16[384,16,96]{0,2,1:T(8,128)(2,1)S(1)}, bf16[384,16,96]{0,2,1:T(8,128)(2,1)}, u32[]{:S(2)}) copy-start(bf16[384,16,96]{0,2,1:T(8,128)(2,1)} %get-tuple-element.81) | copy-start | bytes 3538948
  40.4 1.2 %copy-start.11 = (bf16[12,8,16,128]{3,2,1,0:T(8,128)(2,1)S(1)}, bf16[12,8,16,128]{3,2,1,0:T(8,128)(2,1)}, u32[]{:S(2)}) copy-start(bf16[12,8,16,128]{3,2,1,0:T(8,128)(2,1)} %copy-done.10) | copy-start | bytes 1179652
  41.6 3.5 %copy-start.2 = (bf16[12,8,16,128]{3,2,1,0:T(8,128)(2,1)S(1)}, bf16[12,8,16,128]{3,2,1,0:T(8,128)(2,1)}, u32[]{:S(2)}) copy-start(bf16[12,8,16,128]{3,2,1,0:T(8,128)(2,1)} %copy-done.1) | copy-start | bytes 1179652
  41.6 3.5 %copy-start.7 = (bf16[4,96,16,96]{1,0,3,2:T(4,128)(2,1)S(1)}, bf16[4,96,16,96]{1,0,3,2:T(4,128)(2,1)}, u32[]{:S(2)}) copy-start(bf16[4,96,16,96]{1,0,3,2:T(4,128)(2,1)} %dot_general.70) | copy-start | bytes 3538948
  45.1 1.9 %copy-start.6 = (bf16[4,96,16,96]{1,0,3,2:T(4,128)(2,1)S(1)}, bf16[4,96,16,96]{1,0,3,2:T(4,128)(2,1)}, u32[]{:S(2)}) copy-start(bf16[4,96,16,96]{1,0,3,2:T(4,128)(2,1)} %dot_general.61) | copy-start | bytes 3538948
  45.1 1.9 %copy-start.9 = (bf16[12,8,16,128]{3,2,1,0:T(8,128)(2,1)S(1)}, bf16[12,8,16,128]{3,2,1,0:T(8,128)(2,1)}, u32[]{:S(2)}) copy-start(bf16[12,8,16,128]{3,2,1,0:T(8,128)(2,1)} %copy-done.8) | copy-start | bytes 1179652
  47.1 1.9 %copy-start.5 = (bf16[12,8,16,128]{3,2,1,0:T(8,128)(2,1)S(1)}, bf16[12,8,16,128]{3,2,1,0:T(8,128)(2,1)}, u32[]{:S(2)}) copy-start(bf16[12,8,16,128]{3,2,1,0:T(8,128)(2,1)} %copy-done.3) | copy-start | bytes 1179652
Sparse Core Ops, SparseCore 0:
  52.6 12.1 reduce-scatter.1
where the time goes:
time: 75.7 us; the launch traced here: 75.3 us
  local copies, waits for them, and re-layouts  18 us (24%)
  matrix products  16.3 us (22%)
  between operations  15.9 us (21%)
  waiting for transfers between devices  12.4 us (16%)
  other arithmetic  7 us (9%)
  blocking collectives  4.25 us (6%)
  starting transfers between devices  1.5 us (2%)
    reduce_scatter x1, waiting for transfers between devices, body(): owned = lax.psum_scatter(pair_rank, 'cp', scatter_dimension=0, tiled=True)  9.54 us
    unnamed x56, local copies, waits for them, and re-layouts  5.68 us
    dot_general x2, matrix products, grad_block(): jnp.einsum('hqk,qhd->kd', dscore, query_rows, preferred_element_type=jnp....  5.36 us
    dot_general x2, local copies, waits for them, and re-layouts, grad_block(): jnp.einsum('hqk,qhd->kd', dscore, query_rows, preferred_element_type=jnp....  4.15 us
    dot_general x2, matrix products, grad_block(): jnp.einsum('hqk,qhd->kd', prob_low, grad_rows, preferred_element_type=jnp...  3.83 us
    dot_general x2, matrix products, grad_block(): jnp.einsum('qhd,kd->hqk', grad_rows, value_block, preferred_element_type=...  3.36 us
    dot_general x2, local copies, waits for them, and re-layouts, grad_block(): jnp.einsum('hqk,qhd->kd', prob_low, grad_rows, preferred_element_type=jnp...  3.29 us
    ppermute x1, waiting for transfers between devices, shifted(): return lax.ppermute(block, axis, route)  2.82 us
  transfers between devices with their start and end apart: 2, of which 2 were waited for; matrix products, arithmetic and copies ran while one was open for 24% of the time, Pallas kernels for 0%

commit v1 on v0

v1 whole, which is shorter than its diff:
```python
import functools
import math

import jax
import jax.numpy as jnp
from jax import lax
from jax.experimental import pallas as pl
from jax.experimental.pallas import tpu as pltpu
from jax.sharding import PartitionSpec as P

MESH = pl.DeviceIdType.MESH
NEG = -1e30
LOG2E = math.log2(math.e)


def kernel(
    ranks, sections, block_len,
    pairs, query, keys, values, attn_out, grad_out,
    key_grad, value_grad, upstream,
    q_buf, o_buf, g_buf, k_buf, v_buf, dq_buf, bias, stats, dq_acc, pair_acc, pair_recv,
    in_sem, kv_send, kv_recv, dq_send, dq_recv, pair_send, pair_got,
):
    rows, width = q_buf.shape
    dim = k_buf.shape[1]
    heads = width // dim
    span = rows // 2
    seq = ranks * rows
    blocks = seq // block_len
    scale = 1.0 / math.sqrt(dim)
    me = lax.axis_index("cp")
    sec = lax.axis_index("pp")
    mine = pl.ds(pl.multiple_of(me * rows, rows), rows)

    own = [
        pltpu.make_async_copy(keys, k_buf.at[mine, :], in_sem.at[0]),
        pltpu.make_async_copy(values, v_buf.at[mine, :], in_sem.at[1]),
        pltpu.make_async_copy(query, q_buf, in_sem.at[2]),
        pltpu.make_async_copy(grad_out, g_buf, in_sem.at[3]),
        pltpu.make_async_copy(attn_out, o_buf, in_sem.at[4]),
    ]
    for copy in own:
        copy.start()

    barrier = pltpu.get_barrier_semaphore()
    for off in range(1, ranks):
        pl.semaphore_signal(
            barrier, inc=1, device_id={"cp": lax.rem(me + off, ranks)}, device_id_type=MESH
        )

    @pl.when(sec > 0)
    def _():
        pl.semaphore_signal(barrier, inc=1, device_id={"pp": sec - 1}, device_id_type=MESH)

    @pl.when(sec < sections - 1)
    def _():
        pl.semaphore_signal(barrier, inc=1, device_id={"pp": sec + 1}, device_id_type=MESH)

    row = lax.broadcasted_iota(jnp.int32, (rows, rows), 0)
    col = lax.broadcasted_iota(jnp.int32, (rows, rows), 1)
    q_pos = jnp.where(row < span, pairs[me, 0] * span, pairs[me, 1] * span - span) + row
    for r in range(ranks):
        k_pos = jnp.where(col < span, pairs[r, 0] * span, pairs[r, 1] * span - span) + col
        bias[:, r * rows:(r + 1) * rows] = jnp.where(k_pos <= q_pos, 0.0, NEG)
    pair_acc[...] = jnp.zeros_like(pair_acc)

    pl.semaphore_wait(
        barrier,
        ranks - 1 + (sec > 0).astype(jnp.int32) + (sec < sections - 1).astype(jnp.int32),
    )
    sent = []
    for off in range(1, ranks):
        for which, (src, buf) in enumerate(((keys, k_buf), (values, v_buf))):
            sent.append(
                pltpu.make_async_remote_copy(
                    src_ref=src,
                    dst_ref=buf.at[mine, :],
                    send_sem=kv_send.at[which, off - 1],
                    recv_sem=kv_recv.at[which, off - 1],
                    device_id={"cp": lax.rem(me + off, ranks)},
                    device_id_type=MESH,
                )
            )
    for copy in sent:
        copy.start()

    @pl.when(sec == sections - 1)
    def _():
        upstream[...] = jnp.zeros_like(upstream)

    for copy in own:
        copy.wait()
    for copy in sent:
        copy.wait_recv()

    def dot(a, b, da, db):
        return lax.dot_general(a, b, (((da,), (db,)), ((), ())), preferred_element_type=jnp.float32)

    def send_dq(h):
        lanes = pl.ds(pl.multiple_of(h * dim, dim), dim)
        return pltpu.make_async_remote_copy(
            src_ref=dq_buf.at[:, lanes],
            dst_ref=upstream.at[:, lanes],
            send_sem=dq_send.at[h],
            recv_sem=dq_recv.at[h],
            device_id={"pp": jnp.maximum(sec - 1, 0)},
            device_id_type=MESH,
        )

    def one_head(h, _):
        lanes = pl.ds(pl.multiple_of(h * dim, dim), dim)
        q = q_buf[:, lanes]
        g = g_buf[:, lanes]
        delta = jnp.sum(
            g.astype(jnp.float32) * o_buf[:, lanes].astype(jnp.float32), axis=1, keepdims=True
        )

        def scores(b):
            at = b * block_len if isinstance(b, int) else pl.multiple_of(b * block_len, block_len)
            part = pl.ds(at, block_len)
            return part, dot(q, k_buf[part, :], 1, 1) * (scale * LOG2E) + bias[:, part]

        def terms(part, prob):
            dprob = dot(g, v_buf[part, :], 1, 1)
            dscore = (prob * (dprob - delta) * scale).astype(jnp.bfloat16)
            return prob.astype(jnp.bfloat16), dscore, dot(dscore, k_buf[part, :], 1, 0)

        def pair_terms(part, prob_low, dscore):
            pair_acc[part, :dim] += dot(dscore, q, 0, 0)
            pair_acc[part, dim:] += dot(prob_low, g, 0, 0)

        def start_dq(dq):
            dq_buf[:, lanes] = dq.astype(jnp.bfloat16)

            @pl.when(sec > 0)
            def _():
                send_dq(h).start()

        if blocks == 1:
            part, score = scores(0)
            top = jnp.max(score, axis=1, keepdims=True)
            prob = jnp.exp2(score - top)
            prob = prob * (1.0 / jnp.sum(prob, axis=1, keepdims=True))
            prob_low, dscore, dq = terms(part, prob)
            start_dq(dq)
            pair_terms(part, prob_low, dscore)
        else:
            stats[0] = jnp.full((rows, 1), NEG, jnp.float32)
            stats[1] = jnp.zeros((rows, 1), jnp.float32)
            dq_acc[...] = jnp.zeros_like(dq_acc)

            def gather_stats(b, _):
                _, score = scores(b)
                before = stats[0]
                top = jnp.maximum(before, jnp.max(score, axis=1, keepdims=True))
                mass = jnp.sum(jnp.exp2(score - top), axis=1, keepdims=True)
                stats[1] = stats[1] * jnp.exp2(before - top) + mass
                stats[0] = top
                return 0

            def gather_terms(b, _):
                part, score = scores(b)
                prob = jnp.exp2(score - stats[0]) * (1.0 / stats[1])
                prob_low, dscore, dq = terms(part, prob)
                dq_acc[...] += dq
                pair_terms(part, prob_low, dscore)
                return 0

            lax.fori_loop(0, blocks, gather_stats, 0)
            lax.fori_loop(0, blocks, gather_terms, 0)
            start_dq(dq_acc[...])
        return 0

    lax.fori_loop(0, heads, one_head, 0)

    pair_sent = []
    for off in range(1, ranks):
        dst = lax.rem(me + off, ranks)
        pair_sent.append(
            pltpu.make_async_remote_copy(
                src_ref=pair_acc.at[pl.ds(pl.multiple_of(dst * rows, rows), rows), :],
                dst_ref=pair_recv.at[off - 1],
                send_sem=pair_send.at[off - 1],
                recv_sem=pair_got.at[off - 1],
                device_id={"cp": dst},
                device_id_type=MESH,
            )
        )
    for copy in pair_sent:
        copy.start()
    for copy in sent:
        copy.wait_send()
    for copy in pair_sent:
        copy.wait_recv()
    total = pair_acc[mine, :]
    for off in range(1, ranks):
        total = total + pair_recv[off - 1]
    key_grad[...] = total[:, :dim].astype(jnp.bfloat16)
    value_grad[...] = total[:, dim:].astype(jnp.bfloat16)
    for copy in pair_sent:
        copy.wait_send()

    @pl.when(sec > 0)
    def _():
        for h in range(heads):
            send_dq(h).wait_send()

    @pl.when(sec < sections - 1)
    def _():
        for h in range(heads):
            send_dq(h).wait_recv()


def body(query, keys, values, attn_out, grad_out, span_pairs):
    _, rows, width = query.shape
    dim = keys.shape[2]
    heads = width // dim
    ranks = lax.axis_size("cp")
    sections = lax.axis_size("pp")
    seq = ranks * rows
    block_len = 2 * rows if ranks % 2 == 0 else rows
    low, full = jnp.bfloat16, jnp.float32
    dma = pltpu.SemaphoreType.DMA
    others = max(ranks - 1, 1)
    vmem = pl.BlockSpec(memory_space=pltpu.VMEM)
    hbm = pl.BlockSpec(memory_space=pltpu.HBM)
    key_grad, value_grad, upstream = pl.pallas_call(
        functools.partial(kernel, ranks, sections, block_len),
        out_shape=(
            jax.ShapeDtypeStruct((rows, dim), low),
            jax.ShapeDtypeStruct((rows, dim), low),
            jax.ShapeDtypeStruct((rows, width), low),
        ),
        in_specs=[pl.BlockSpec(memory_space=pltpu.SMEM)] + [hbm] * 5,
        out_specs=(vmem, vmem, vmem),
        scratch_shapes=[
            pltpu.VMEM((rows, width), low),
            pltpu.VMEM((rows, width), low),
            pltpu.VMEM((rows, width), low),
            pltpu.VMEM((seq, dim), low),
            pltpu.VMEM((seq, dim), low),
            pltpu.VMEM((rows, width), low),
            pltpu.VMEM((rows, seq), full),
            pltpu.VMEM((2, rows, 1), full),
            pltpu.VMEM((rows, dim), full),
            pltpu.VMEM((seq, 2 * dim), full),
            pltpu.VMEM((others, rows, 2 * dim), full),
            dma((5,)),
            dma((2, others)),
            dma((2, others)),
            dma((heads,)),
            dma((heads,)),
            dma((others,)),
            dma((others,)),
        ],
        compiler_params=pltpu.CompilerParams(
            collective_id=0, has_side_effects=True, vmem_limit_bytes=48 * 1024 * 1024
        ),
        name="backward",
    )(span_pairs, query[0], keys[0], values[0], attn_out[0], grad_out[0])
    return key_grad[None], value_grad[None], upstream[None]


def solution(mesh):
    spec = P("pp", "cp", "tp")
    return jax.shard_map(
        body,
        mesh=mesh,
        in_specs=(spec, spec, spec, spec, spec, P()),
        out_specs=(spec, spec, spec),
        check_vma=False,
    )
```

time: 75.7 us -> 33.5 us (0.44)
  Pallas kernels: 0 us -> 24.7 us
  matrix products: 16.3 us -> 0 us
  between operations: 15.9 us -> 0.65 us
  waiting for transfers between devices: 12.4 us -> 0 us
  local copies, waits for them, and re-layouts: 18 us -> 7.79 us
  other arithmetic: 7 us -> 0 us
  blocking collectives: 4.25 us -> 0 us
  starting transfers between devices: 1.5 us -> 0 us
    pallas_call x0 -> x1, Pallas kernels: none -> 24.7 us  [body(): pl.pallas_call(functools.partial(kernel, ranks, sections, block_len), out...]
    dot_general x10 -> x0, matrix products: 16.3 us -> none  [the longest x2 5.36 us: grad_block(): jnp.einsum('hqk,qhd->kd', dscore, query_rows, preferred_element_type=jnp....]
    reduce_scatter x1 -> x0, waiting for transfers between devices: 9.54 us -> none  [body(): owned = lax.psum_scatter(pair_rank, 'cp', scatter_dimension=0, tiled=True)]
    dot_general x6 -> x0, local copies, waits for them, and re-layouts: 7.55 us -> none  [the longest x2 4.15 us: grad_block(): jnp.einsum('hqk,qhd->kd', dscore, query_rows, preferred_element_type=jnp....]
    all_gather x2 -> x0, blocking collectives: 4.25 us -> none  [the longest x1 2.18 us: body(): lax.all_gather(keys[0], 'cp', axis=0, tiled=True)]
    ppermute x1 -> x0, waiting for transfers between devices: 2.82 us -> none  [shifted(): return lax.ppermute(block, axis, route)]
    unnamed x56 -> x15, local copies, waits for them, and re-layouts: 5.68 us -> 7.79 us
    reduce_sum x3 -> x0, other arithmetic: 1.88 us -> none  [the longest x2 1.8 us: stats_step(): jnp.sum(jnp.exp(score - top_next[:, :, None]), axis=-1)]
  transfers between devices with their start and end apart: 2 -> 0, of which waited for: 2 -> 0; matrix products, arithmetic and copies ran while one was open for 24% -> 0% of each run, Pallas kernels for 0% -> 0%
where the time goes in v1:
time: 33.5 us; the launch traced here: 33.1 us
  Pallas kernels  24.7 us (74%)
  local copies, waits for them, and re-layouts  7.79 us (23%)
  between operations  0.65 us (2%)
    pallas_call x1, Pallas kernels, body(): pl.pallas_call(functools.partial(kernel, ranks, sections, block_len), out...  24.7 us
    unnamed x15, local copies, waits for them, and re-layouts  7.79 us

profile of v1, /device:TPU:0, one launch (start us, length us, event | category | flops | bytes accessed | tf_op | source)
XLA Modules:
  0.0 33.1 jit_solution(3254401178100335021)
XLA Ops:
  0.6 0.0 copy-start.5
  0.6 0.7 %copy-done.5 = s32[2,2]{1,0:T(2,128)S(1)} copy-done((s32[2,2]{1,0:T(2,128)S(1)}, s32[2,2]{1,0:T(2,128)}, u32[]{:S(2)}) %copy-start.5) | copy-done | bytes 40
  1.3 0.0 copy-start
  1.3 1.1 %copy-done = bf16[1,192,2048]{2,1,0:T(8,128)(2,1)S(1)} copy-done((bf16[1,192,2048]{2,1,0:T(8,128)(2,1)S(1)}, bf16[1,192,2048]{2,1,0:T(8,128)(2,1)}, u32[]{:S(2)}) %copy-start) | copy-done | bytes 786456
  2.4 0.0 copy-start.1
  2.4 1.1 %copy-done.1 = bf16[1,192,2048]{2,1,0:T(8,128)(2,1)S(1)} copy-done((bf16[1,192,2048]{2,1,0:T(8,128)(2,1)S(1)}, bf16[1,192,2048]{2,1,0:T(8,128)(2,1)}, u32[]{:S(2)}) %copy-start.1) | copy-done | bytes 786456
  3.6 0.0 copy-start.2
  3.6 1.1 %copy-done.2 = bf16[1,192,2048]{2,1,0:T(8,128)(2,1)S(1)} copy-done((bf16[1,192,2048]{2,1,0:T(8,128)(2,1)S(1)}, bf16[1,192,2048]{2,1,0:T(8,128)(2,1)}, u32[]{:S(2)}) %copy-start.2) | copy-done | bytes 786456
  4.7 0.0 copy-start.3
  4.7 0.8 %copy-done.3 = bf16[1,192,128]{2,1,0:T(8,128)(2,1)S(1)} copy-done((bf16[1,192,128]{2,1,0:T(8,128)(2,1)S(1)}, bf16[1,192,128]{2,1,0:T(8,128)(2,1)}, u32[]{:S(2)}) %copy-start.3) | copy-done | bytes 49176
  5.5 0.0 copy-start.4
  5.5 0.8 %copy-done.4 = bf16[1,192,128]{2,1,0:T(8,128)(2,1)S(1)} copy-done((bf16[1,192,128]{2,1,0:T(8,128)(2,1)S(1)}, bf16[1,192,128]{2,1,0:T(8,128)(2,1)}, u32[]{:S(2)}) %copy-start.4) | copy-done | bytes 49176
  6.3 24.7 %backward.1 = (bf16[192,128]{1,0:T(8,128)(2,1)S(1)}, bf16[192,128]{1,0:T(8,128)(2,1)S(1)}, bf16[192,2048]{1,0:T(8,128)(2,1)S(1)}) custom-call(s32[2,2]{1,0:T(2,128)S(1)} %copy-done.5, bf16[192,2048]{1,0:T(8,128)(2,1)S(1)} %bitcast.9, bf16[192,128]{1,0:T(8,128)(2,1)S(1)} %bitcast.14, bf16[192,128]{1,0:T(8,128)(2,1)S(1)} %bitcast.15, ...), custom_call_target="tpu_custom_call" | custom-call | tf_op jit(solution)/shard_map/backward/pallas_call | solution.py:226
  31.0 0.6 %copy.12 = bf16[1,192,128]{2,1,0:T(8,128)(2,1)} copy(bf16[1,192,128]{2,1,0:T(8,128)(2,1)S(1)} %bitcast.13) | data formatting | bytes 98304
  31.7 0.6 %copy.13 = bf16[1,192,128]{2,1,0:T(8,128)(2,1)} copy(bf16[1,192,128]{2,1,0:T(8,128)(2,1)S(1)} %bitcast.12) | data formatting | bytes 98304
  32.3 0.9 %copy.14 = bf16[1,192,2048]{2,1,0:T(8,128)(2,1)} copy(bf16[1,192,2048]{2,1,0:T(8,128)(2,1)S(1)} %bitcast.8) | data formatting | bytes 1572864
Async XLA Ops:
  0.6 0.7 %copy-start.5 = (s32[2,2]{1,0:T(2,128)S(1)}, s32[2,2]{1,0:T(2,128)}, u32[]{:S(2)}) copy-start(s32[2,2]{1,0:T(2,128)} %pairs.1) | copy-start | bytes 52
  1.3 1.1 %copy-start = (bf16[1,192,2048]{2,1,0:T(8,128)(2,1)S(1)}, bf16[1,192,2048]{2,1,0:T(8,128)(2,1)}, u32[]{:S(2)}) copy-start(bf16[1,192,2048]{2,1,0:T(8,128)(2,1)} %param.6) | copy-start | bytes 2359300
  2.4 1.1 %copy-start.1 = (bf16[1,192,2048]{2,1,0:T(8,128)(2,1)S(1)}, bf16[1,192,2048]{2,1,0:T(8,128)(2,1)}, u32[]{:S(2)}) copy-start(bf16[1,192,2048]{2,1,0:T(8,128)(2,1)} %param.9) | copy-start | bytes 2359300
  3.6 1.1 %copy-start.2 = (bf16[1,192,2048]{2,1,0:T(8,128)(2,1)S(1)}, bf16[1,192,2048]{2,1,0:T(8,128)(2,1)}, u32[]{:S(2)}) copy-start(bf16[1,192,2048]{2,1,0:T(8,128)(2,1)} %param.10) | copy-start | bytes 2359300
  4.7 0.8 %copy-start.3 = (bf16[1,192,128]{2,1,0:T(8,128)(2,1)S(1)}, bf16[1,192,128]{2,1,0:T(8,128)(2,1)}, u32[]{:S(2)}) copy-start(bf16[1,192,128]{2,1,0:T(8,128)(2,1)} %param.7) | copy-start | bytes 147460
  5.5 0.8 %copy-start.4 = (bf16[1,192,128]{2,1,0:T(8,128)(2,1)S(1)}, bf16[1,192,128]{2,1,0:T(8,128)(2,1)}, u32[]{:S(2)}) copy-start(bf16[1,192,128]{2,1,0:T(8,128)(2,1)} %param.8) | copy-start | bytes 147460

commit v2 on v1

--- a/solution.py
+++ b/solution.py
@@ -210,6 +210,19 @@
             send_dq(h).wait_recv()
 
 
+def store(key_grad, value_grad, upstream, key_out, value_out, upstream_out, sem):
+    copies = [
+        pltpu.make_async_copy(src, dst, sem.at[i])
+        for i, (src, dst) in enumerate(
+            ((upstream, upstream_out), (key_grad, key_out), (value_grad, value_out))
+        )
+    ]
+    for copy in copies:
+        copy.start()
+    for copy in copies:
+        copy.wait()
+
+
 def body(query, keys, values, attn_out, grad_out, span_pairs):
     _, rows, width = query.shape
     dim = keys.shape[2]
@@ -226,9 +239,9 @@
     key_grad, value_grad, upstream = pl.pallas_call(
         functools.partial(kernel, ranks, sections, block_len),
         out_shape=(
-            jax.ShapeDtypeStruct((rows, dim), low),
-            jax.ShapeDtypeStruct((rows, dim), low),
-            jax.ShapeDtypeStruct((rows, width), low),
+            pltpu.VMEM((rows, dim), low),
+            pltpu.VMEM((rows, dim), low),
+            pltpu.VMEM((rows, width), low),
         ),
         in_specs=[pl.BlockSpec(memory_space=pltpu.SMEM)] + [hbm] * 5,
         out_specs=(vmem, vmem, vmem),
@@ -253,10 +266,24 @@
             dma((others,)),
         ],
         compiler_params=pltpu.CompilerParams(
-            collective_id=0, has_side_effects=True, vmem_limit_bytes=48 * 1024 * 1024
+            collective_id=0, has_side_effects=True, vmem_limit_bytes=64 * 1024 * 1024 - 1200 * 1024
         ),
         name="backward",
     )(span_pairs, query[0], keys[0], values[0], attn_out[0], grad_out[0])
+    anywhere = pl.BlockSpec(memory_space=pl.ANY)
+    key_grad, value_grad, upstream = pl.pallas_call(
+        store,
+        out_shape=(
+            jax.ShapeDtypeStruct((rows, dim), low),
+            jax.ShapeDtypeStruct((rows, dim), low),
+            jax.ShapeDtypeStruct((rows, width), low),
+        ),
+        in_specs=[anywhere] * 3,
+        out_specs=(anywhere,) * 3,
+        scratch_shapes=[dma((3,))],
+        compiler_params=pltpu.CompilerParams(vmem_limit_bytes=1024 * 1024),
+        name="store",
+    )(key_grad, value_grad, upstream)
     return key_grad[None], value_grad[None], upstream[None]
 
 

time: 33.5 us -> 26.5 us (0.79)
  local copies, waits for them, and re-layouts: 7.79 us -> 0 us
  Pallas kernels: 24.7 us -> 25.7 us
    unnamed x15 -> x0, local copies, waits for them, and re-layouts: 7.79 us -> none
    pallas_call x0 -> x1, Pallas kernels: none -> 0.92 us  [body(): pl.pallas_call(store, out_shape=(jax.ShapeDtypeStruct((rows, dim), low),...]
where the time goes in v2:
time: 26.5 us; the launch traced here: 26.4 us
  Pallas kernels  25.7 us (97%)
  between operations  0.64 us (2%)
    pallas_call x1, Pallas kernels, body(): pl.pallas_call(functools.partial(kernel, ranks, sections, block_len), out...  24.8 us
    pallas_call x1, Pallas kernels, body(): pl.pallas_call(store, out_shape=(jax.ShapeDtypeStruct((rows, dim), low),...  0.92 us

profile of v2, /device:TPU:0, one launch (start us, length us, event | category | flops | bytes accessed | tf_op | source)
XLA Modules:
  0.0 26.4 jit_solution(16173932530222112032)
XLA Ops:
  0.6 24.8 %backward.1 = (bf16[192,128]{1,0:T(8,128)(2,1)S(1)}, bf16[192,128]{1,0:T(8,128)(2,1)S(1)}, bf16[192,2048]{1,0:T(8,128)(2,1)S(1)}) custom-call(s32[2,2]{1,0:T(2,128)} %pairs.1, bf16[192,2048]{1,0:T(8,128)(2,1)} %bitcast.8, bf16[192,128]{1,0:T(8,128)(2,1)} %bitcast.11, bf16[192,128]{1,0:T(8,128)(2,1)} %bitcast.12, bf16[192,2048]{1,0:T(8,128)(2,1)} %bitcast.9, ...), custom_call_target="tpu_custom_call" | custom-call | tf_op jit(solution)/shard_map/backward/pallas_call | solution.py:239
  25.4 0.9 %store.1 = (bf16[192,128]{1,0:T(8,128)(2,1)}, bf16[192,128]{1,0:T(8,128)(2,1)}, bf16[192,2048]{1,0:T(8,128)(2,1)}) custom-call(bf16[192,128]{1,0:T(8,128)(2,1)S(1)} %get-tuple-element.9.key_grad, bf16[192,128]{1,0:T(8,128)(2,1)S(1)} %get-tuple-element.10.value_grad, bf16[192,2048]{1,0:T(8,128)(2,1)S(1)} %get-tuple-element.11.upstream), custom_call_target="tpu_custom_call" | custom-call | tf_op jit(solution)/shard_map/store/pallas_call | solution.py:274

commit v3 on v2

--- a/solution.py
+++ b/solution.py
@@ -13,24 +13,22 @@
 LOG2E = math.log2(math.e)
 
 
-def kernel(
-    ranks, sections, block_len,
+def gather(
+    ranks,
     pairs, query, keys, values, attn_out, grad_out,
-    key_grad, value_grad, upstream,
-    q_buf, o_buf, g_buf, k_buf, v_buf, dq_buf, bias, stats, dq_acc, pair_acc, pair_recv,
-    in_sem, kv_send, kv_recv, dq_send, dq_recv, pair_send, pair_got,
+    q_buf, o_buf, g_buf, k_buf, v_buf, bias,
+    in_sem, kv_send, kv_recv,
 ):
-    rows, width = q_buf.shape
-    dim = k_buf.shape[1]
-    heads = width // dim
+    rows = q_buf.shape[0]
     span = rows // 2
-    seq = ranks * rows
-    blocks = seq // block_len
-    scale = 1.0 / math.sqrt(dim)
     me = lax.axis_index("cp")
-    sec = lax.axis_index("pp")
     mine = pl.ds(pl.multiple_of(me * rows, rows), rows)
 
+    barrier = pltpu.get_barrier_semaphore()
+    for off in range(1, ranks):
+        pl.semaphore_signal(
+            barrier, inc=1, device_id={"cp": lax.rem(me + off, ranks)}, device_id_type=MESH
+        )
     own = [
         pltpu.make_async_copy(keys, k_buf.at[mine, :], in_sem.at[0]),
         pltpu.make_async_copy(values, v_buf.at[mine, :], in_sem.at[1]),
@@ -40,33 +38,7 @@
     ]
     for copy in own:
         copy.start()
-
-    barrier = pltpu.get_barrier_semaphore()
-    for off in range(1, ranks):
-        pl.semaphore_signal(
-            barrier, inc=1, device_id={"cp": lax.rem(me + off, ranks)}, device_id_type=MESH
-        )
-
-    @pl.when(sec > 0)
-    def _():
-        pl.semaphore_signal(barrier, inc=1, device_id={"pp": sec - 1}, device_id_type=MESH)
-
-    @pl.when(sec < sections - 1)
-    def _():
-        pl.semaphore_signal(barrier, inc=1, device_id={"pp": sec + 1}, device_id_type=MESH)
-
-    row = lax.broadcasted_iota(jnp.int32, (rows, rows), 0)
-    col = lax.broadcasted_iota(jnp.int32, (rows, rows), 1)
-    q_pos = jnp.where(row < span, pairs[me, 0] * span, pairs[me, 1] * span - span) + row
-    for r in range(ranks):
-        k_pos = jnp.where(col < span, pairs[r, 0] * span, pairs[r, 1] * span - span) + col
-        bias[:, r * rows:(r + 1) * rows] = jnp.where(k_pos <= q_pos, 0.0, NEG)
-    pair_acc[...] = jnp.zeros_like(pair_acc)
-
-    pl.semaphore_wait(
-        barrier,
-        ranks - 1 + (sec > 0).astype(jnp.int32) + (sec < sections - 1).astype(jnp.int32),
-    )
+    pl.semaphore_wait(barrier, ranks - 1)
     sent = []
     for off in range(1, ranks):
         for which, (src, buf) in enumerate(((keys, k_buf), (values, v_buf))):
@@ -83,20 +55,66 @@
     for copy in sent:
         copy.start()
 
-    @pl.when(sec == sections - 1)
-    def _():
-        upstream[...] = jnp.zeros_like(upstream)
+    row = lax.broadcasted_iota(jnp.int32, (rows, rows), 0)
+    col = lax.broadcasted_iota(jnp.int32, (rows, rows), 1)
+    q_pos = jnp.where(row < span, pairs[me, 0] * span, pairs[me, 1] * span - span) + row
+    for r in range(ranks):
+        k_pos = jnp.where(col < span, pairs[r, 0] * span, pairs[r, 1] * span - span) + col
+        bias[:, r * rows:(r + 1) * rows] = jnp.where(k_pos <= q_pos, 0.0, NEG)
 
     for copy in own:
         copy.wait()
     for copy in sent:
-        copy.wait_recv()
+        copy.wait()
+
+
+def kernel(
+    ranks, sections, block_len,
+    q_buf, o_buf, g_buf, k_buf, v_buf, bias,
+    key_grad, value_grad, upstream,
+    dq_buf, stats, dq_acc, pair_acc, pair_recv,
+    dq_send, dq_recv, pair_send, pair_got,
+):
+    rows, width = q_buf.shape
+    dim = k_buf.shape[1]
+    heads = width // dim
+    seq = ranks * rows
+    blocks = seq // block_len
+    scale = 1.0 / math.sqrt(dim)
+    me = lax.axis_index("cp")
+    sec = lax.axis_index("pp")
+    mine = pl.ds(pl.multiple_of(me * rows, rows), rows)
+
+    barrier = pltpu.get_barrier_semaphore()
+    for off in range(1, ranks):
+        pl.semaphore_signal(
+            barrier, inc=1, device_id={"cp": lax.rem(me + off, ranks)}, device_id_type=MESH
+        )
+
+    @pl.when(sec > 0)
+    def _():
+        pl.semaphore_signal(barrier, inc=1, device_id={"pp": sec - 1}, device_id_type=MESH)
+
+    @pl.when(sec < sections - 1)
+    def _():
+        pl.semaphore_signal(barrier, inc=1, device_id={"pp": sec + 1}, device_id_type=MESH)
+
+    pair_acc[...] = jnp.zeros_like(pair_acc)
 
     def dot(a, b, da, db):
         return lax.dot_general(a, b, (((da,), (db,)), ((), ())), preferred_element_type=jnp.float32)
 
+    def enter():
+        pl.semaphore_wait(
+            barrier,
+            ranks - 1 + (sec > 0).astype(jnp.int32) + (sec < sections - 1).astype(jnp.int32),
+        )
+
+    def lanes_of(h):
+        return pl.ds(h * dim if isinstance(h, int) else pl.multiple_of(h * dim, dim), dim)
+
     def send_dq(h):
-        lanes = pl.ds(pl.multiple_of(h * dim, dim), dim)
+        lanes = lanes_of(h)
         return pltpu.make_async_remote_copy(
             src_ref=dq_buf.at[:, lanes],
             dst_ref=upstream.at[:, lanes],
@@ -107,7 +125,7 @@
         )
 
     def one_head(h, _):
-        lanes = pl.ds(pl.multiple_of(h * dim, dim), dim)
+        lanes = lanes_of(h)
         q = q_buf[:, lanes]
         g = g_buf[:, lanes]
         delta = jnp.sum(
@@ -130,6 +148,9 @@
 
         def start_dq(dq):
             dq_buf[:, lanes] = dq.astype(jnp.bfloat16)
+
+            if isinstance(h, int):
+                enter()
 
             @pl.when(sec > 0)
             def _():
@@ -170,7 +191,13 @@
             start_dq(dq_acc[...])
         return 0
 
-    lax.fori_loop(0, heads, one_head, 0)
+    one_head(0, 0)
+
+    @pl.when(sec == sections - 1)
+    def _():
+        upstream[...] = jnp.zeros_like(upstream)
+
+    lax.fori_loop(1, heads, one_head, 0)
 
     pair_sent = []
     for off in range(1, ranks):
@@ -187,8 +214,6 @@
         )
     for copy in pair_sent:
         copy.start()
-    for copy in sent:
-        copy.wait_send()
     for copy in pair_sent:
         copy.wait_recv()
     total = pair_acc[mine, :]
@@ -236,6 +261,28 @@
     others = max(ranks - 1, 1)
     vmem = pl.BlockSpec(memory_space=pltpu.VMEM)
     hbm = pl.BlockSpec(memory_space=pltpu.HBM)
+    gathered = (
+        ((rows, width), low),
+        ((rows, width), low),
+        ((rows, width), low),
+        ((seq, dim), low),
+        ((seq, dim), low),
+        ((rows, seq), full),
+    )
+    held = sum(math.prod(shape) * jnp.dtype(kind).itemsize for shape, kind in gathered)
+    inputs = pl.pallas_call(
+        functools.partial(gather, ranks),
+        out_shape=tuple(pltpu.VMEM(shape, kind) for shape, kind in gathered),
+        in_specs=[pl.BlockSpec(memory_space=pltpu.SMEM)] + [hbm] * 5,
+        out_specs=(vmem,) * 6,
+        scratch_shapes=[dma((5,)), dma((2, others)), dma((2, others))],
+        compiler_params=pltpu.CompilerParams(
+            collective_id=1,
+            has_side_effects=True,
+            vmem_limit_bytes=64 * 1024 * 1024 - held - 128 * 1024,
+        ),
+        name="gather",
+    )(span_pairs, query[0], keys[0], values[0], attn_out[0], grad_out[0])
     key_grad, value_grad, upstream = pl.pallas_call(
         functools.partial(kernel, ranks, sections, block_len),
         out_shape=(
@@ -243,33 +290,24 @@
             pltpu.VMEM((rows, dim), low),
             pltpu.VMEM((rows, width), low),
         ),
-        in_specs=[pl.BlockSpec(memory_space=pltpu.SMEM)] + [hbm] * 5,
+        in_specs=[vmem] * 6,
         out_specs=(vmem, vmem, vmem),
         scratch_shapes=[
             pltpu.VMEM((rows, width), low),
-            pltpu.VMEM((rows, width), low),
-            pltpu.VMEM((rows, width), low),
-            pltpu.VMEM((seq, dim), low),
-            pltpu.VMEM((seq, dim), low),
-            pltpu.VMEM((rows, width), low),
-            pltpu.VMEM((rows, seq), full),
             pltpu.VMEM((2, rows, 1), full),
             pltpu.VMEM((rows, dim), full),
             pltpu.VMEM((seq, 2 * dim), full),
             pltpu.VMEM((others, rows, 2 * dim), full),
-            dma((5,)),
-            dma((2, others)),
-            dma((2, others)),
             dma((heads,)),
             dma((heads,)),
             dma((others,)),
             dma((others,)),
         ],
         compiler_params=pltpu.CompilerParams(
-            collective_id=0, has_side_effects=True, vmem_limit_bytes=64 * 1024 * 1024 - 1200 * 1024
+            collective_id=0, has_side_effects=True, vmem_limit_bytes=32 * 1024 * 1024
         ),
         name="backward",
-    )(span_pairs, query[0], keys[0], values[0], attn_out[0], grad_out[0])
+    )(*inputs)
     anywhere = pl.BlockSpec(memory_space=pl.ANY)
     key_grad, value_grad, upstream = pl.pallas_call(
         store,

time: 26.5 us -> 26.7 us (level)
    pallas_call x0 -> x1, Pallas kernels: none -> 2.48 us  [body(): pl.pallas_call(functools.partial(gather, ranks), out_shape=tuple((pltpu.V...]
    pallas_call x1, Pallas kernels: 24.8 us -> 22.5 us  [body(): pl.pallas_call(functools.partial(kernel, ranks, sections, block_len), out...]
where the time goes in v3:
time: 26.7 us; the launch traced here: 26.5 us
  Pallas kernels  25.9 us (97%)
  between operations  0.65 us (2%)
    pallas_call x1, Pallas kernels, body(): pl.pallas_call(functools.partial(kernel, ranks, sections, block_len), out...  22.5 us
    pallas_call x1, Pallas kernels, body(): pl.pallas_call(functools.partial(gather, ranks), out_shape=tuple((pltpu.V...  2.48 us
    pallas_call x1, Pallas kernels, body(): pl.pallas_call(store, out_shape=(jax.ShapeDtypeStruct((rows, dim), low),...  0.92 us

profile of v3, /device:TPU:0, one launch (start us, length us, event | category | flops | bytes accessed | tf_op | source)
XLA Modules:
  0.0 26.5 jit_solution(6667434441836700646)
XLA Ops:
  0.6 2.5 %gather.1 = (bf16[192,2048]{1,0:T(8,128)(2,1)S(1)}, bf16[192,2048]{1,0:T(8,128)(2,1)S(1)}, bf16[192,2048]{1,0:T(8,128)(2,1)S(1)}, bf16[384,128]{1,0:T(8,128)(2,1...) custom-call(s32[2,2]{1,0:T(2,128)} %pairs.1, bf16[192,2048]{1,0:T(8,128)(2,1)} %bitcast.8, ...), custom_call_target="tpu_custom_call" | custom-call | tf_op jit(solution)/shard_map/gather/pallas_call | solution.py:273
  3.1 22.5 %backward.1 = (bf16[192,128]{1,0:T(8,128)(2,1)S(1)}, bf16[192,128]{1,0:T(8,128)(2,1)S(1)}, bf16[192,2048]{1,0:T(8,128)(2,1)S(1)}) custom-call(bf16[192,2048]{1,0:T(8,128)(2,1)S(1)} %get-tuple-element.15.q_buf, bf16[192,2048]{1,0:T(8,128)(2,1)S(1)} %get-tuple-element.16.o_buf, bf16[192,2048]{1,0:T(8,128)(2,1)S(1)} %get-tuple-element.17.g_buf, ...), custom_call_target="tpu_custom_call" | custom-call | tf_op jit(solution)/shard_map/backward/pallas_call | solution.py:286
  25.6 0.9 %store.1 = (bf16[192,128]{1,0:T(8,128)(2,1)}, bf16[192,128]{1,0:T(8,128)(2,1)}, bf16[192,2048]{1,0:T(8,128)(2,1)}) custom-call(bf16[192,128]{1,0:T(8,128)(2,1)S(1)} %get-tuple-element.21.key_grad, bf16[192,128]{1,0:T(8,128)(2,1)S(1)} %get-tuple-element.22.value_grad, bf16[192,2048]{1,0:T(8,128)(2,1)S(1)} %get-tuple-element.23.upstream), custom_call_target="tpu_custom_call" | custom-call | tf_op jit(solution)/shard_map/store/pallas_call | solution.py:312

commit v4 on v2

--- a/solution.py
+++ b/solution.py
@@ -29,17 +29,7 @@
     scale = 1.0 / math.sqrt(dim)
     me = lax.axis_index("cp")
     sec = lax.axis_index("pp")
-    mine = pl.ds(pl.multiple_of(me * rows, rows), rows)
-
-    own = [
-        pltpu.make_async_copy(keys, k_buf.at[mine, :], in_sem.at[0]),
-        pltpu.make_async_copy(values, v_buf.at[mine, :], in_sem.at[1]),
-        pltpu.make_async_copy(query, q_buf, in_sem.at[2]),
-        pltpu.make_async_copy(grad_out, g_buf, in_sem.at[3]),
-        pltpu.make_async_copy(attn_out, o_buf, in_sem.at[4]),
-    ]
-    for copy in own:
-        copy.start()
+    mine = pl.ds(0, rows)
 
     barrier = pltpu.get_barrier_semaphore()
     for off in range(1, ranks):
@@ -47,47 +37,54 @@
             barrier, inc=1, device_id={"cp": lax.rem(me + off, ranks)}, device_id_type=MESH
         )
 
-    @pl.when(sec > 0)
-    def _():
-        pl.semaphore_signal(barrier, inc=1, device_id={"pp": sec - 1}, device_id_type=MESH)
-
     @pl.when(sec < sections - 1)
     def _():
         pl.semaphore_signal(barrier, inc=1, device_id={"pp": sec + 1}, device_id_type=MESH)
 
-    row = lax.broadcasted_iota(jnp.int32, (rows, rows), 0)
-    col = lax.broadcasted_iota(jnp.int32, (rows, rows), 1)
-    q_pos = jnp.where(row < span, pairs[me, 0] * span, pairs[me, 1] * span - span) + row
-    for r in range(ranks):
-        k_pos = jnp.where(col < span, pairs[r, 0] * span, pairs[r, 1] * span - span) + col
-        bias[:, r * rows:(r + 1) * rows] = jnp.where(k_pos <= q_pos, 0.0, NEG)
-    pair_acc[...] = jnp.zeros_like(pair_acc)
-
-    pl.semaphore_wait(
-        barrier,
-        ranks - 1 + (sec > 0).astype(jnp.int32) + (sec < sections - 1).astype(jnp.int32),
-    )
+    own = [
+        pltpu.make_async_copy(keys, k_buf.at[mine, :], in_sem.at[0]),
+        pltpu.make_async_copy(values, v_buf.at[mine, :], in_sem.at[1]),
+    ]
+    first, rest = pl.ds(0, dim), pl.ds(dim, width - dim)
+    wide = ((query, q_buf), (grad_out, g_buf), (attn_out, o_buf))
+    begin = [
+        pltpu.make_async_copy(src.at[:, first], dst.at[:, first], in_sem.at[2 + i])
+        for i, (src, dst) in enumerate(wide)
+    ]
+    later = [
+        pltpu.make_async_copy(src.at[:, rest], dst.at[:, rest], in_sem.at[5 + i])
+        for i, (src, dst) in enumerate(wide)
+    ]
+    for copy in own + begin:
+        copy.start()
+
+    pl.semaphore_wait(barrier, ranks - 1 + (sec > 0).astype(jnp.int32))
     sent = []
     for off in range(1, ranks):
         for which, (src, buf) in enumerate(((keys, k_buf), (values, v_buf))):
             sent.append(
                 pltpu.make_async_remote_copy(
                     src_ref=src,
-                    dst_ref=buf.at[mine, :],
+                    dst_ref=buf.at[pl.ds((ranks - off) * rows, rows), :],
                     send_sem=kv_send.at[which, off - 1],
                     recv_sem=kv_recv.at[which, off - 1],
                     device_id={"cp": lax.rem(me + off, ranks)},
                     device_id_type=MESH,
                 )
             )
-    for copy in sent:
+    for copy in sent + later:
         copy.start()
 
-    @pl.when(sec == sections - 1)
-    def _():
-        upstream[...] = jnp.zeros_like(upstream)
-
-    for copy in own:
+    row = lax.broadcasted_iota(jnp.int32, (rows, rows), 0)
+    col = lax.broadcasted_iota(jnp.int32, (rows, rows), 1)
+    q_pos = jnp.where(row < span, pairs[me, 0] * span, pairs[me, 1] * span - span) + row
+    for r in range(ranks):
+        rank = lax.rem(me + r, ranks)
+        k_pos = jnp.where(col < span, pairs[rank, 0] * span, pairs[rank, 1] * span - span) + col
+        bias[:, r * rows:(r + 1) * rows] = jnp.where(k_pos <= q_pos, 0.0, NEG)
+    pair_acc[...] = jnp.zeros_like(pair_acc)
+
+    for copy in own + begin:
         copy.wait()
     for copy in sent:
         copy.wait_recv()
@@ -95,29 +92,31 @@
     def dot(a, b, da, db):
         return lax.dot_general(a, b, (((da,), (db,)), ((), ())), preferred_element_type=jnp.float32)
 
-    def send_dq(h):
-        lanes = pl.ds(pl.multiple_of(h * dim, dim), dim)
+    def lanes_of(h):
+        return pl.ds(h * dim if isinstance(h, int) else pl.multiple_of(h * dim, dim), dim)
+
+    def send_dq(h, lines, slot):
         return pltpu.make_async_remote_copy(
-            src_ref=dq_buf.at[:, lanes],
-            dst_ref=upstream.at[:, lanes],
-            send_sem=dq_send.at[h],
-            recv_sem=dq_recv.at[h],
+            src_ref=dq_buf.at[lines, lanes_of(h)],
+            dst_ref=upstream.at[lines, lanes_of(h)],
+            send_sem=dq_send.at[slot],
+            recv_sem=dq_recv.at[slot],
             device_id={"pp": jnp.maximum(sec - 1, 0)},
             device_id_type=MESH,
         )
 
-    def one_head(h, _):
-        lanes = pl.ds(pl.multiple_of(h * dim, dim), dim)
-        q = q_buf[:, lanes]
-        g = g_buf[:, lanes]
+    def rows_of_head(h, lines, slot):
+        lanes = lanes_of(h)
+        q = q_buf[lines, lanes]
+        g = g_buf[lines, lanes]
         delta = jnp.sum(
-            g.astype(jnp.float32) * o_buf[:, lanes].astype(jnp.float32), axis=1, keepdims=True
+            g.astype(jnp.float32) * o_buf[lines, lanes].astype(jnp.float32), axis=1, keepdims=True
         )
 
         def scores(b):
             at = b * block_len if isinstance(b, int) else pl.multiple_of(b * block_len, block_len)
             part = pl.ds(at, block_len)
-            return part, dot(q, k_buf[part, :], 1, 1) * (scale * LOG2E) + bias[:, part]
+            return part, dot(q, k_buf[part, :], 1, 1) * (scale * LOG2E) + bias[lines, part]
 
         def terms(part, prob):
             dprob = dot(g, v_buf[part, :], 1, 1)
@@ -129,11 +128,11 @@
             pair_acc[part, dim:] += dot(prob_low, g, 0, 0)
 
         def start_dq(dq):
-            dq_buf[:, lanes] = dq.astype(jnp.bfloat16)
+            dq_buf[lines, lanes] = dq.astype(jnp.bfloat16)
 
             @pl.when(sec > 0)
             def _():
-                send_dq(h).start()
+                send_dq(h, lines, slot).start()
 
         if blocks == 1:
             part, score = scores(0)
@@ -144,40 +143,54 @@
             start_dq(dq)
             pair_terms(part, prob_low, dscore)
         else:
-            stats[0] = jnp.full((rows, 1), NEG, jnp.float32)
-            stats[1] = jnp.zeros((rows, 1), jnp.float32)
-            dq_acc[...] = jnp.zeros_like(dq_acc)
+            stats[0, lines] = jnp.full((lines.size, 1), NEG, jnp.float32)
+            stats[1, lines] = jnp.zeros((lines.size, 1), jnp.float32)
+            dq_acc[lines] = jnp.zeros((lines.size, dim), jnp.float32)
 
             def gather_stats(b, _):
                 _, score = scores(b)
-                before = stats[0]
+                before = stats[0, lines]
                 top = jnp.maximum(before, jnp.max(score, axis=1, keepdims=True))
                 mass = jnp.sum(jnp.exp2(score - top), axis=1, keepdims=True)
-                stats[1] = stats[1] * jnp.exp2(before - top) + mass
-                stats[0] = top
+                stats[1, lines] = stats[1, lines] * jnp.exp2(before - top) + mass
+                stats[0, lines] = top
                 return 0
 
             def gather_terms(b, _):
                 part, score = scores(b)
-                prob = jnp.exp2(score - stats[0]) * (1.0 / stats[1])
+                prob = jnp.exp2(score - stats[0, lines]) * (1.0 / stats[1, lines])
                 prob_low, dscore, dq = terms(part, prob)
-                dq_acc[...] += dq
+                dq_acc[lines] += dq
                 pair_terms(part, prob_low, dscore)
                 return 0
 
             lax.fori_loop(0, blocks, gather_stats, 0)
             lax.fori_loop(0, blocks, gather_terms, 0)
-            start_dq(dq_acc[...])
+            start_dq(dq_acc[lines])
+
+    pieces = [(h, pl.ds(0, rows), h) for h in range(heads)]
+    for piece in pieces[:1]:
+        rows_of_head(*piece)
+
+    @pl.when(sec == sections - 1)
+    def _():
+        upstream[...] = jnp.zeros_like(upstream)
+
+    for copy in later:
+        copy.wait()
+
+    def one_head(h, _):
+        rows_of_head(h, pl.ds(0, rows), h)
         return 0
 
-    lax.fori_loop(0, heads, one_head, 0)
+    lax.fori_loop(1, heads, one_head, 0)
 
     pair_sent = []
     for off in range(1, ranks):
         dst = lax.rem(me + off, ranks)
         pair_sent.append(
             pltpu.make_async_remote_copy(
-                src_ref=pair_acc.at[pl.ds(pl.multiple_of(dst * rows, rows), rows), :],
+                src_ref=pair_acc.at[pl.ds(off * rows, rows), :],
                 dst_ref=pair_recv.at[off - 1],
                 send_sem=pair_send.at[off - 1],
                 recv_sem=pair_got.at[off - 1],
@@ -201,13 +214,13 @@
 
     @pl.when(sec > 0)
     def _():
-        for h in range(heads):
-            send_dq(h).wait_send()
+        for piece in pieces:
+            send_dq(*piece).wait_send()
 
     @pl.when(sec < sections - 1)
     def _():
-        for h in range(heads):
-            send_dq(h).wait_recv()
+        for piece in pieces:
+            send_dq(*piece).wait_recv()
 
 
 def store(key_grad, value_grad, upstream, key_out, value_out, upstream_out, sem):
@@ -257,11 +270,11 @@
             pltpu.VMEM((rows, dim), full),
             pltpu.VMEM((seq, 2 * dim), full),
             pltpu.VMEM((others, rows, 2 * dim), full),
-            dma((5,)),
+            dma((8,)),
             dma((2, others)),
             dma((2, others)),
-            dma((heads,)),
-            dma((heads,)),
+            dma((heads + 1,)),
+            dma((heads + 1,)),
             dma((others,)),
             dma((others,)),
         ],

time: 26.5 us -> 25.7 us (0.970)
  Pallas kernels: 25.7 us -> 24.9 us
    pallas_call x1, Pallas kernels: 24.8 us -> 24 us  [body(): pl.pallas_call(functools.partial(kernel, ranks, sections, block_len), out...]
where the time goes in v4:
time: 25.7 us; the launch traced here: 25.6 us
  Pallas kernels  24.9 us (97%)
  between operations  0.64 us (2%)
    pallas_call x1, Pallas kernels, body(): pl.pallas_call(functools.partial(kernel, ranks, sections, block_len), out...  24 us
    pallas_call x1, Pallas kernels, body(): pl.pallas_call(store, out_shape=(jax.ShapeDtypeStruct((rows, dim), low),...  0.92 us

profile of v4, /device:TPU:0, one launch (start us, length us, event | category | flops | bytes accessed | tf_op | source)
XLA Modules:
  0.0 25.6 jit_solution(2101403710307463405)
XLA Ops:
  0.6 24.0 %backward.1 = (bf16[192,128]{1,0:T(8,128)(2,1)S(1)}, bf16[192,128]{1,0:T(8,128)(2,1)S(1)}, bf16[192,2048]{1,0:T(8,128)(2,1)S(1)}) custom-call(s32[2,2]{1,0:T(2,128)} %pairs.1, bf16[192,2048]{1,0:T(8,128)(2,1)} %bitcast.8, bf16[192,128]{1,0:T(8,128)(2,1)} %bitcast.11, bf16[192,128]{1,0:T(8,128)(2,1)} %bitcast.12, bf16[192,2048]{1,0:T(8,128)(2,1)} %bitcast.9, ...), custom_call_target="tpu_custom_call" | custom-call | tf_op jit(solution)/shard_map/backward/pallas_call | solution.py:252
  24.6 0.9 %store.1 = (bf16[192,128]{1,0:T(8,128)(2,1)}, bf16[192,128]{1,0:T(8,128)(2,1)}, bf16[192,2048]{1,0:T(8,128)(2,1)}) custom-call(bf16[192,128]{1,0:T(8,128)(2,1)S(1)} %get-tuple-element.9.key_grad, bf16[192,128]{1,0:T(8,128)(2,1)S(1)} %get-tuple-element.10.value_grad, bf16[192,2048]{1,0:T(8,128)(2,1)S(1)} %get-tuple-element.11.upstream), custom_call_target="tpu_custom_call" | custom-call | tf_op jit(solution)/shard_map/store/pallas_call | solution.py:287

commit v5 on v4

--- a/solution.py
+++ b/solution.py
@@ -15,10 +15,10 @@
 
 def kernel(
     ranks, sections, block_len,
-    pairs, query, keys, values, attn_out, grad_out,
+    pairs_hbm, query, keys, values, attn_out, grad_out,
     key_grad, value_grad, upstream,
     q_buf, o_buf, g_buf, k_buf, v_buf, dq_buf, bias, stats, dq_acc, pair_acc, pair_recv,
-    in_sem, kv_send, kv_recv, dq_send, dq_recv, pair_send, pair_got,
+    pairs, in_sem, kv_send, kv_recv, dq_send, dq_recv, pair_send, pair_got,
 ):
     rows, width = q_buf.shape
     dim = k_buf.shape[1]
@@ -55,7 +55,8 @@
         pltpu.make_async_copy(src.at[:, rest], dst.at[:, rest], in_sem.at[5 + i])
         for i, (src, dst) in enumerate(wide)
     ]
-    for copy in own + begin:
+    table = pltpu.make_async_copy(pairs_hbm, pairs, in_sem.at[8])
+    for copy in [table] + own + begin:
         copy.start()
 
     pl.semaphore_wait(barrier, ranks - 1 + (sec > 0).astype(jnp.int32))
@@ -75,6 +76,7 @@
     for copy in sent + later:
         copy.start()
 
+    table.wait()
     row = lax.broadcasted_iota(jnp.int32, (rows, rows), 0)
     col = lax.broadcasted_iota(jnp.int32, (rows, rows), 1)
     q_pos = jnp.where(row < span, pairs[me, 0] * span, pairs[me, 1] * span - span) + row
@@ -256,7 +258,7 @@
             pltpu.VMEM((rows, dim), low),
             pltpu.VMEM((rows, width), low),
         ),
-        in_specs=[pl.BlockSpec(memory_space=pltpu.SMEM)] + [hbm] * 5,
+        in_specs=[hbm] * 6,
         out_specs=(vmem, vmem, vmem),
         scratch_shapes=[
             pltpu.VMEM((rows, width), low),
@@ -270,7 +272,8 @@
             pltpu.VMEM((rows, dim), full),
             pltpu.VMEM((seq, 2 * dim), full),
             pltpu.VMEM((others, rows, 2 * dim), full),
-            dma((8,)),
+            pltpu.SMEM((ranks, 2), jnp.int32),
+            dma((9,)),
             dma((2, others)),
             dma((2, others)),
             dma((heads + 1,)),

time: 25.7 us -> 25 us (0.973)
  Pallas kernels: 24.9 us -> 24.2 us
    pallas_call x1, Pallas kernels: 24 us -> 23.3 us  [body(): pl.pallas_call(functools.partial(kernel, ranks, sections, block_len), out...]
where the time goes in v5:
time: 25 us; the launch traced here: 24.9 us
  Pallas kernels  24.2 us (97%)
  between operations  0.64 us (3%)
    pallas_call x1, Pallas kernels, body(): pl.pallas_call(functools.partial(kernel, ranks, sections, block_len), out...  23.3 us
    pallas_call x1, Pallas kernels, body(): pl.pallas_call(store, out_shape=(jax.ShapeDtypeStruct((rows, dim), low),...  0.92 us

profile of v5, /device:TPU:0, one launch (start us, length us, event | category | flops | bytes accessed | tf_op | source)
XLA Modules:
  0.0 24.9 jit_solution(17606763144967410101)
XLA Ops:
  0.6 23.3 %backward.1 = (bf16[192,128]{1,0:T(8,128)(2,1)S(1)}, bf16[192,128]{1,0:T(8,128)(2,1)S(1)}, bf16[192,2048]{1,0:T(8,128)(2,1)S(1)}) custom-call(s32[2,2]{1,0:T(2,128)} %pairs_hbm.1, bf16[192,2048]{1,0:T(8,128)(2,1)} %bitcast.8, bf16[192,128]{1,0:T(8,128)(2,1)} %bitcast.11, bf16[192,128]{1,0:T(8,128)(2,1)} %bitcast.12, bf16[192,2048]{1,0:T(8,128)(2,1)} %bitcast.9, ...), custom_call_target="tpu_custom_call" | custom-call | tf_op jit(solution)/shard_map/backward/pallas_call | solution.py:254
  23.9 0.9 %store.1 = (bf16[192,128]{1,0:T(8,128)(2,1)}, bf16[192,128]{1,0:T(8,128)(2,1)}, bf16[192,2048]{1,0:T(8,128)(2,1)}) custom-call(bf16[192,128]{1,0:T(8,128)(2,1)S(1)} %get-tuple-element.9.key_grad, bf16[192,128]{1,0:T(8,128)(2,1)S(1)} %get-tuple-element.10.value_grad, bf16[192,2048]{1,0:T(8,128)(2,1)S(1)} %get-tuple-element.11.upstream), custom_call_target="tpu_custom_call" | custom-call | tf_op jit(solution)/shard_map/store/pallas_call | solution.py:290
